TPU v7x, 128 devices: a whole 4x4x4 slice. The times are simulated.
128 devices in a mesh: tm: 16 (over z, x), space: 8 (over y, core).
Axes of the slice: x: 4, y: 4, z: 4, core: 2. Of those that a mesh axis runs over, the one named last changes fastest.
Arguments:
- ensembles: bfloat16 [256, 80, 16384], P('tm', None, 'space'), may hold values from -6 to 6
- cotangents: bfloat16 [256, 80, 16384], P('tm', None, 'space'), may hold values from -6 to 6
- transforms: float32 [256, 80, 80], P('tm'), may hold values from -1.5 to 1.5
Outputs:
- smoothed: bfloat16 [256, 80, 16384], P('tm', None, 'space')
- ensemble_grad: bfloat16 [256, 80, 16384], P('tm', None, 'space')
- transform_grad: float32 [256, 80, 80], P('tm')
All inputs are finite; a program needn't handle non-finite values.
Results may differ from a plain program's by a relative error of at most 0.0049.
Values sent between devices are 32-bit elements; how exact they have to be, the bound alone decides.
A program may use at most 64 MiB of HBM per device.

v0:
```python
import functools
import math

import jax
import jax.numpy as jnp
from jax import lax
from jax.experimental import pallas as pl
from jax.experimental.pallas import tpu as pltpu
from jax.sharding import PartitionSpec as P

MESH = pl.DeviceIdType.MESH
f32 = jnp.float32
bf16 = jnp.bfloat16


def mm(a, b, dims=((1,), (0,))):
    return lax.dot_general(
        a, b, (dims, ((), ())), precision=lax.Precision.HIGHEST, preferred_element_type=f32
    )


def block_scans(tr, count, prefix_ref, suffix_ref):
    groups = count // 4
    heads, tails = [], []
    for g in range(groups):
        w = [tr[4 * g + i] for i in range(4)]
        w01, w23 = mm(w[0], w[1]), mm(w[2], w[3])
        heads.append((w[0], w01, mm(w01, w[2]), mm(w01, w23)))
        tails.append((None, mm(w[1], w23), w23, w[3]))
    before = None
    for g in range(groups):
        for i in range(4):
            if g == 0 and i == 0:
                continue
            if i == 0:
                prefix_ref[4 * g] = before
            elif g == 0:
                prefix_ref[i] = heads[0][i - 1]
            else:
                prefix_ref[4 * g + i] = mm(before, heads[g][i - 1])
        before = heads[g][3] if g == 0 else mm(before, heads[g][3])
    after = None
    for g in reversed(range(groups)):
        whole = heads[g][3]
        parts = (whole,) + tails[g][1:]
        for i in range(4):
            suffix_ref[4 * g + i] = parts[i] if after is None else mm(parts[i], after)
        after = whole if after is None else mm(whole, after)


def block_total(tr, count):
    level = [tr[i] for i in range(count)]
    while len(level) > 1:
        level = [mm(level[i], level[i + 1]) for i in range(0, len(level), 2)]
    return level[0]


def exchange_kernel(
    n_tm, n_sp, times, members,
    e_hbm, c_hbm, t_hbm,
    e_v, c_v, lt_out, pre_out, prod_out, mt_out,
    tr, p_own, p_buf, ltp, lt_rx, lt_core, lt_ry, lt_fin, ot_own, ot_rx, ot_buf, mt_buf, suf,
    in_sem, p_s, p_r, pf_s, pf_r, lp_s, lp_r, ly_s, ly_r, la_s, la_r, lf_s, lf_r,
    or_s, or_r, ot_s, ot_r, mx_s, mx_r,
):
    half = members // 2
    n_y = n_sp // 2
    per_core = times // 2
    own = per_core // n_y
    me = lax.axis_index("tm")
    sp = lax.axis_index("space")
    y = sp // 2
    c = lax.rem(sp, 2)
    partner = 2 * y + (1 - c)

    def tm_peer(d):
        return lax.rem(me + d, n_tm)

    def sp_peer(d):
        return lax.rem(sp + d, n_sp)

    def remote(src, dst, s_sem, r_sem, device):
        return pltpu.make_async_remote_copy(
            src_ref=src, dst_ref=dst, send_sem=s_sem, recv_sem=r_sem,
            device_id=device, device_id_type=MESH,
        )

    t_copy = pltpu.make_async_copy(t_hbm, tr, in_sem.at[2 * times])
    t_copy.start()
    loads = []
    for t in range(times):
        loads.append((
            pltpu.make_async_copy(e_hbm.at[t], e_v.at[t], in_sem.at[t]),
            pltpu.make_async_copy(c_hbm.at[t], c_v.at[t], in_sem.at[times + t]),
        ))
        for copy in loads[-1]:
            copy.start()

    barrier = pltpu.get_barrier_semaphore()
    for d in range(1, n_tm):
        pl.semaphore_signal(barrier, inc=1, device_id={"tm": tm_peer(d)}, device_id_type=MESH)
    for d in range(1, n_sp):
        pl.semaphore_signal(barrier, inc=1, device_id={"space": sp_peer(d)}, device_id_type=MESH)

    t_copy.wait()
    total = block_total(tr, times)
    p_own[0] = total[:half]
    p_own[1] = total[half:]
    p_buf[c, me] = p_own[c]

    pl.semaphore_wait(barrier, n_tm - 1 + n_sp - 1)

    p_copies = []
    for d in range(1, n_tm):
        copy = remote(p_own.at[c], p_buf.at[c, me], p_s.at[d], p_r.at[d], {"tm": tm_peer(d)})
        copy.start()
        p_copies.append(copy)

    lp_copies = []
    waiting = []
    state = None
    for pair in range(times // 2 + 1):
        if pair < times // 2:
            for t in (2 * pair, 2 * pair + 1):
                for copy in loads[t]:
                    copy.wait()
            fresh = [
                lax.dot_general(
                    c_v[t], e_v[t], (((1,), (1,)), ((), ())), preferred_element_type=f32
                )
                for t in (2 * pair, 2 * pair + 1)
            ]
        else:
            fresh = []
        if pair > 0:
            for k, gram in enumerate(waiting):
                t = 2 * (pair - 1) + k
                state = gram if t == 0 else gram + mm(state, tr[t - 1])
                ltp[t] = state
            j = pair - 1
            copy = remote(
                ltp.at[2 * j + 1 - c], lt_rx.at[j], lp_s.at[j], lp_r.at[j], {"space": partner}
            )
            copy.start()
            lp_copies.append(copy)
        waiting = fresh

    leaving = mm(state, tr[times - 1])
    ot_own[0] = leaving[:half]
    ot_own[1] = leaving[half:]
    or_copies = []
    for d in range(1, n_sp):
        peer = sp_peer(d)
        copy = remote(
            ot_own.at[lax.rem(peer, 2)], ot_rx.at[d], or_s.at[d], or_r.at[d], {"space": peer}
        )
        copy.start()
        or_copies.append(copy)

    for j in range(per_core):
        lp_copies[j].wait_recv()
        lt_core[j] = ltp[2 * j + c] + lt_rx[j]
    ly_copies = []
    for d in range(1, n_y):
        q = lax.rem(y + d, n_y)
        copy = remote(
            lt_core.at[pl.ds(q * own, own)], lt_ry.at[d], ly_s.at[d], ly_r.at[d],
            {"space": 2 * q + c},
        )
        copy.start()
        ly_copies.append(copy)

    block_scans(tr, times, pre_out, suf)

    pf_copies = []
    own_copy = remote(
        p_own.at[c], p_buf.at[c, me], pf_s.at[0], pf_r.at[0], {"space": partner}
    )
    own_copy.start()
    pf_copies.append(own_copy)

    summed = ot_own[c]
    for d in range(1, n_sp):
        or_copies[d - 1].wait_recv()
        summed = summed + ot_rx[d]
    ot_buf[me] = summed
    ot_copies = []
    for d in range(1, n_tm):
        copy = remote(ot_buf.at[me], ot_buf.at[me], ot_s.at[d], ot_r.at[d], {"tm": tm_peer(d)})
        copy.start()
        ot_copies.append(copy)

    for d in range(1, n_tm):
        p_copies[d - 1].wait_recv()
        source = lax.rem(me + n_tm - d, n_tm)
        copy = remote(
            p_buf.at[c, source], p_buf.at[c, source], pf_s.at[d], pf_r.at[d], {"space": partner}
        )
        copy.start()
        pf_copies.append(copy)

    mine = [lt_core[y * own + k] for k in range(own)]
    for d in range(1, n_y):
        ly_copies[d - 1].wait_recv()
        mine = [mine[k] + lt_ry[d, k] for k in range(own)]
    for k in range(own):
        lt_fin[c, y, k] = mine[k]
    la_copies = []
    for d in range(1, n_y):
        q = lax.rem(y + d, n_y)
        copy = remote(
            lt_fin.at[c, y], lt_fin.at[c, y], la_s.at[d], la_r.at[d], {"space": 2 * q + c}
        )
        copy.start()
        la_copies.append(copy)
    lf_copies = []
    copy = remote(lt_fin.at[c, y], lt_fin.at[c, y], lf_s.at[0], lf_r.at[0], {"space": partner})
    copy.start()
    lf_copies.append(copy)

    for copy in pf_copies:
        copy.wait_recv()

    rows = lax.broadcasted_iota(jnp.int32, (members, members), 0)
    cols = lax.broadcasted_iota(jnp.int32, (members, members), 1)
    later = jnp.where(rows == cols, 1.0, 0.0).astype(f32)
    for b in reversed(range(1, n_tm)):
        whole = jnp.concatenate([p_buf[0, b], p_buf[1, b]], axis=0)
        later = jnp.where(b > me, mm(whole, later), later)
    for t in range(times):
        prod_out[t] = mm(suf[t], later)
    prod_out[times] = later

    for d in range(1, n_y):
        la_copies[d - 1].wait_recv()
        q = lax.rem(y + n_y - d, n_y)
        copy = remote(lt_fin.at[c, q], lt_fin.at[c, q], lf_s.at[d], lf_r.at[d], {"space": partner})
        copy.start()
        lf_copies.append(copy)

    for copy in ot_copies:
        copy.wait_recv()
    entering = jnp.zeros((half, members), f32)
    for b in range(n_tm - 1):
        whole = jnp.concatenate([p_buf[0, b], p_buf[1, b]], axis=0)
        entering = jnp.where(b < me, mm(entering, whole) + ot_buf[b], entering)
    mt_buf[c] = entering
    mx_copy = remote(mt_buf.at[c], mt_buf.at[c], mx_s.at[0], mx_r.at[0], {"space": partner})
    mx_copy.start()

    for copy in lf_copies:
        copy.wait_recv()
    for k in range(2):
        for q in range(n_y):
            for i in range(own):
                lt_out[2 * (q * own + i) + k] = lt_fin[k, q, i]
    mx_copy.wait_recv()
    mt_out[:half] = mt_buf[0]
    mt_out[half:] = mt_buf[1]

    for copy in (
        p_copies + lp_copies + or_copies + ly_copies + pf_copies
        + ot_copies + la_copies + lf_copies + [mx_copy]
    ):
        copy.wait_send()


def output_kernel(
    times, scale,
    e_v, c_v, lt, pre, prod, mt,
    sm_hbm, eg_hbm, tg_hbm,
    sm, eg, tg, sems, tg_sem,
):
    copies = []
    for t in range(times):
        factor = prod[t].astype(bf16)
        sm[t] = lax.dot_general(
            factor, e_v[t], (((0,), (0,)), ((), ())), preferred_element_type=f32
        ).astype(bf16)
        eg[t] = jnp.dot(factor, c_v[t], preferred_element_type=f32).astype(bf16)
        for k, (src, dst) in enumerate(((sm, sm_hbm), (eg, eg_hbm))):
            copy = pltpu.make_async_copy(src.at[t], dst.at[t], sems.at[k, t])
            copy.start()
            copies.append(copy)
    entering = mt[...]
    for t in range(times):
        total = lt[t] + (entering if t == 0 else mm(entering, pre[t]))
        tg[t] = mm(total, prod[t + 1], ((0,), (1,))) * scale
    copy = pltpu.make_async_copy(tg, tg_hbm, tg_sem)
    copy.start()
    copies.append(copy)
    for copy in copies:
        copy.wait()


def shards(n_tm, n_sp, ensembles, cotangents, transforms):
    times, members, cells = ensembles.shape
    half = members // 2
    n_y = n_sp // 2
    per_core = times // 2
    own = per_core // n_y
    square = (members, members)
    halves = (half, members)
    anywhere = pl.BlockSpec(memory_space=pl.ANY)
    vmem = pl.BlockSpec(memory_space=pltpu.VMEM)
    dma = pltpu.SemaphoreType.DMA
    shape = jax.ShapeDtypeStruct
    big = shape((times, members, cells), bf16)
    stack = shape((times,) + square, f32)
    e_v, c_v, lt, pre, prod, mt = pl.pallas_call(
        functools.partial(exchange_kernel, n_tm, n_sp, times, members),
        out_shape=[big, big, stack, stack, shape((times + 1,) + square, f32), shape(square, f32)],
        in_specs=[pl.BlockSpec(memory_space=pltpu.HBM)] * 3,
        out_specs=[vmem] * 6,
        scratch_shapes=[
            pltpu.VMEM((times,) + square, f32),
            pltpu.VMEM((2,) + halves, f32),
            pltpu.VMEM((2, n_tm) + halves, f32),
            pltpu.VMEM((times,) + square, f32),
            pltpu.VMEM((per_core,) + square, f32),
            pltpu.VMEM((per_core,) + square, f32),
            pltpu.VMEM((n_y, own) + square, f32),
            pltpu.VMEM((2, n_y, own) + square, f32),
            pltpu.VMEM((2,) + halves, f32),
            pltpu.VMEM((n_sp,) + halves, f32),
            pltpu.VMEM((n_tm,) + halves, f32),
            pltpu.VMEM((2,) + halves, f32),
            pltpu.VMEM((times,) + square, f32),
            dma((2 * times + 1,)),
            dma((n_tm,)), dma((n_tm,)),
            dma((n_tm,)), dma((n_tm,)),
            dma((per_core,)), dma((per_core,)),
            dma((n_y,)), dma((n_y,)),
            dma((n_y,)), dma((n_y,)),
            dma((n_y,)), dma((n_y,)),
            dma((n_sp,)), dma((n_sp,)),
            dma((n_tm,)), dma((n_tm,)),
            dma((1,)), dma((1,)),
        ],
        compiler_params=pltpu.CompilerParams(
            collective_id=0, has_side_effects=True, vmem_limit_bytes=24 * 2**20
        ),
        name="exchange",
    )(*(pltpu.with_memory_space_constraint(a, pltpu.HBM) for a in (ensembles, cotangents, transforms)))
    scale = 1.0 / math.sqrt(cells * n_sp * times * n_tm)
    return pl.pallas_call(
        functools.partial(output_kernel, times, scale),
        out_shape=[big, big, stack],
        in_specs=[vmem] * 6,
        out_specs=[anywhere] * 3,
        scratch_shapes=[
            pltpu.VMEM((times, members, cells), bf16),
            pltpu.VMEM((times, members, cells), bf16),
            pltpu.VMEM((times,) + square, f32),
            dma((2, times)),
            dma(()),
        ],
        compiler_params=pltpu.CompilerParams(vmem_limit_bytes=30 * 2**20),
        name="outputs",
    )(e_v, c_v, lt, pre, prod, mt)


def solution(mesh):
    specs = (P("tm", None, "space"), P("tm", None, "space"), P("tm", None, None))
    return jax.shard_map(
        functools.partial(shards, mesh.shape["tm"], mesh.shape["space"]),
        mesh=mesh,
        in_specs=specs,
        out_specs=specs,
        check_vma=False,
    )
```

profile of v0, /device:TPU:1, one launch (start us, length us, event | category | flops | bytes accessed | tf_op | source)
XLA Modules:
  0.0 41.6 jit_solution(2962604847985800511)
XLA Ops:
  0.6 33.7 %exchange.1 = (bf16[16,80,2048]{2,1,0:T(8,128)(2,1)S(1)}, bf16[16,80,2048]{2,1,0:T(8,128)(2,1)S(1)}, f32[16,80,80]{2,1,0:T(8,128)S(1)}, f32[16,80,80]{2,1,0:T(8,...) custom-call(bf16[16,80,2048]{2,1,0:T(8,128)(2,1)} %e_hbm.1, bf16[16,80,2048]{2,1,0:T(8,128)(2,1)} %c_hbm.1, ...), custom_call_target="tpu_custom_call" | custom-call | tf_op jit(solution)/shard_map/exchange/pallas_call | solution.py:310
  34.3 7.1 %outputs.1 = (bf16[16,80,2048]{2,1,0:T(8,128)(2,1)}, bf16[16,80,2048]{2,1,0:T(8,128)(2,1)}, f32[16,80,80]{2,1,0:T(8,128)}) custom-call(bf16[16,80,2048]{2,1,0:T(8,128)(2,1)S(1)} %get-tuple-element.9.e_v, bf16[16,80,2048]{2,1,0:T(8,128)(2,1)S(1)} %get-tuple-element.10.c_v, f32[16,80,80]{2,1,0:T(8,128)S(1)} %get-tuple-element.11.lt, ...), custom_call_target="tpu_custom_call" | custom-call | tf_op jit(solution)/shard_map/outputs/pallas_call | solution.py:346
where the time goes:
time: 41.7 us; the launch traced here: 41.6 us
  Pallas kernels  40.8 us (98%)
  between operations  0.8 us (2%)
    pallas_call x1, Pallas kernels, shards(): pl.pallas_call(functools.partial(exchange_kernel, n_tm, n_sp, times, memb...  33.7 us
    pallas_call x1, Pallas kernels, shards(): pl.pallas_call(functools.partial(output_kernel, times, scale), out_shape=...  7.08 us

commit v1 on v0

v1 whole, which is shorter than its diff:
```python
import functools
import math

import jax
import jax.numpy as jnp
from jax import lax
from jax.experimental import pallas as pl
from jax.experimental.pallas import tpu as pltpu
from jax.sharding import PartitionSpec as P

MESH = pl.DeviceIdType.MESH
PB, PF, OR, OT, OF, LP, LY, LA, LF = range(9)
f32 = jnp.float32
bf16 = jnp.bfloat16


def mm(a, b, dims=((1,), (0,))):
    return lax.dot_general(
        a, b, (dims, ((), ())), precision=lax.Precision.HIGHEST, preferred_element_type=f32
    )


def group_scans(tr, groups):
    heads, tails = [], []
    for g in range(groups):
        w = [tr[4 * g + i] for i in range(4)]
        w01, w23 = mm(w[0], w[1]), mm(w[2], w[3])
        heads.append((w[0], w01, mm(w01, w[2]), mm(w01, w23)))
        tails.append((None, mm(w[1], w23), w23, w[3]))
    return heads, tails


def block_scans(heads, tails, prefix_ref, suffix_ref):
    groups = len(heads)
    before = None
    for g in range(groups):
        for i in range(4):
            if g == 0 and i == 0:
                continue
            if i == 0:
                prefix_ref[4 * g] = before
            elif g == 0:
                prefix_ref[i] = heads[0][i - 1]
            else:
                prefix_ref[4 * g + i] = mm(before, heads[g][i - 1])
        before = heads[g][3] if g == 0 else mm(before, heads[g][3])
    after = None
    for g in reversed(range(groups)):
        whole = heads[g][3]
        parts = (whole,) + tails[g][1:]
        for i in range(4):
            suffix_ref[4 * g + i] = parts[i] if after is None else mm(parts[i], after)
        after = whole if after is None else mm(whole, after)


def block_total(tr, count):
    level = [tr[i] for i in range(count)]
    while len(level) > 1:
        level = [mm(level[i], level[i + 1]) for i in range(0, len(level), 2)]
    return level[0]


def pack(square):
    rows = square.shape[0]
    left, rest, tall = 64, rows - 64, rows // 5
    wide = jnp.concatenate([square[: rows // 2, :left], square[rows // 2 :, :left]], axis=1)
    pieces = [square[tall * g : tall * (g + 1), left:] for g in range(5)]
    pieces.append(jnp.zeros((tall, 2 * left - 5 * rest), f32))
    return jnp.concatenate([wide, jnp.concatenate(pieces, axis=1)], axis=0)


def unpack(packed, rows):
    left, rest, tall = 64, rows - 64, rows // 5
    wide, tail = packed[: rows // 2], packed[rows // 2 :]
    first = jnp.concatenate([wide[:, :left], wide[:, left:]], axis=0)
    last = jnp.concatenate([tail[:, rest * g : rest * (g + 1)] for g in range(5)], axis=0)
    return jnp.concatenate([first, last], axis=1)


def exchange_kernel(
    n_tm, n_sp, times, members,
    e_hbm, c_hbm, t_hbm,
    sm_v, eg_v, lt_out, pre_out, prod_out, p_out, ot_out,
    e_v, c_v, tr, p_own, p_buf, ltp, lt_rx, lt_core, lt_ry, lt_fin, ot_own, ot_rx, ot_buf, suf, scan_buf, gram, carry,
    in_sem, s_sem, r_sem, lp_r, ly_r, la_r, lf_r,
):
    half = members // 2
    n_y = n_sp // 2
    own = times // 2 // n_y
    batch = times // own
    me = lax.axis_index("tm")
    sp = lax.axis_index("space")
    y = sp // 2
    c = lax.rem(sp, 2)
    partner = 2 * y + (1 - c)

    def tm_peer(d):
        return lax.rem(me + d, n_tm)

    def sp_peer(d):
        return lax.rem(sp + d, n_sp)

    def send(src, dst, sems, device):
        pltpu.make_async_remote_copy(
            src_ref=src, dst_ref=dst, send_sem=sems[0], recv_sem=sems[1],
            device_id=device, device_id_type=MESH,
        ).start()

    def wait(ref, sem):
        pltpu.make_async_copy(ref, ref, sem).wait()

    t_copy = pltpu.make_async_copy(t_hbm, tr, in_sem.at[10])
    t_copy.start()
    groups = [(0, 4), (4, 8), (8, 12), (12, 14), (14, 16)]
    loads = []
    for g, (first, last) in enumerate(groups):
        part = pl.ds(first, last - first)
        loads.append((
            pltpu.make_async_copy(e_hbm.at[part], e_v.at[part], in_sem.at[2 * g]),
            pltpu.make_async_copy(c_hbm.at[part], c_v.at[part], in_sem.at[2 * g + 1]),
        ))
        for copy in loads[-1]:
            copy.start()

    barrier = pltpu.get_barrier_semaphore()
    for d in range(1, n_tm):
        pl.semaphore_signal(barrier, inc=1, device_id={"tm": tm_peer(d)}, device_id_type=MESH)
    for d in range(1, n_sp):
        pl.semaphore_signal(barrier, inc=1, device_id={"space": sp_peer(d)}, device_id_type=MESH)

    t_copy.wait()
    total = block_total(tr, times)
    p_own[0] = total[:half]
    p_own[1] = total[half:]
    p_buf[c, me] = p_own[c]

    def send_pairs(first, last):
        k = first // n_y
        part = pl.ds(first, last - first)
        send(ltp.at[1 - c, part], lt_rx.at[part], (s_sem.at[LP], lp_r.at[k]), {"space": partner})

    def reduce_cores(k):
        wait(lt_rx.at[pl.ds(k * n_y, n_y)], lp_r.at[k])
        for j in range(k * n_y, (k + 1) * n_y):
            lt_core[j] = ltp[c, j] + lt_rx[j]
        for d in range(1, n_y):
            q = lax.rem(y + d, n_y)
            send(
                lt_core.at[k * n_y + q], lt_ry.at[k, d - 1], (s_sem.at[LY], ly_r.at[k]),
                {"space": 2 * q + c},
            )

    def hand_round(k):
        wait(lt_ry.at[k], ly_r.at[k])
        mine = lt_core[k * n_y + y]
        for d in range(1, n_y):
            mine = mine + lt_ry[k, d - 1]
        lt_fin[k, c, y] = mine
        for d in range(1, n_y):
            q = lax.rem(y + d, n_y)
            send(
                lt_fin.at[k, c, y], lt_fin.at[k, c, y], (s_sem.at[LA], la_r.at[k]),
                {"space": 2 * q + c},
            )

    def forward_totals(k):
        wait(lt_ry.at[k], la_r.at[k])
        send(lt_fin.at[k, c], lt_fin.at[k, c], (s_sem.at[LF], lf_r.at[k]), {"space": partner})

    before = (0, 0)
    for g, (first, last) in enumerate(groups + [(times, times)]):
        if last > first:
            for copy in loads[g]:
                copy.wait()
        if before[0]:
            state = carry[...]
        for k in range(max(last - first, before[1] - before[0])):
            if first + k < last:
                t = first + k
                gram[t] = lax.dot_general(
                    c_v[t], e_v[t], (((1,), (1,)), ((), ())), preferred_element_type=f32
                )
            if before[0] + k < before[1]:
                t = before[0] + k
                state = gram[t] if t == 0 else gram[t] + mm(state, tr[t - 1])
                ltp[t % 2, t // 2] = pack(state)
        if before[1]:
            carry[...] = state
        if before[1]:
            send_pairs(before[0] // 2, before[1] // 2)
        before = (first, last)
        if g == 0:
            pl.semaphore_wait(barrier, n_tm - 1 + n_sp - 1)
            for d in range(1, n_tm):
                send(p_own.at[c], p_buf.at[c, me], (s_sem.at[PB], r_sem.at[PB]), {"tm": tm_peer(d)})

    leaving = mm(carry[...], tr[times - 1])
    ot_own[0] = leaving[:half]
    ot_own[1] = leaving[half:]
    for d in range(1, n_sp):
        peer = sp_peer(d)
        send(
            ot_own.at[lax.rem(peer, 2)], ot_rx.at[d - 1], (s_sem.at[OR], r_sem.at[OR]),
            {"space": peer},
        )

    reduce_cores(0)
    heads, tails = group_scans(tr, times // 4)
    for g in range(times // 4):
        for i in range(1, 4):
            scan_buf[g, i - 1] = heads[g][i]
        for i in range(1, 3):
            scan_buf[g, 2 + i] = tails[g][i]
    for k in range(1, own):
        reduce_cores(k)
    heads = [
        (tr[4 * g], scan_buf[g, 0], scan_buf[g, 1], scan_buf[g, 2]) for g in range(times // 4)
    ]
    tails = [
        (None, scan_buf[g, 3], scan_buf[g, 4], tr[4 * g + 3]) for g in range(times // 4)
    ]
    block_scans(heads, tails, pre_out, suf)

    wait(p_buf.at[c, pl.ds(0, n_tm - 1)], r_sem.at[PB])
    send(p_buf.at[c], p_buf.at[c], (s_sem.at[PF], r_sem.at[PF]), {"space": partner})

    wait(ot_rx, r_sem.at[OR])
    summed = ot_own[c]
    for d in range(1, n_sp):
        summed = summed + ot_rx[d - 1]
    ot_buf[c, me] = summed
    for d in range(1, n_tm):
        send(
            ot_buf.at[c, me], ot_buf.at[c, me], (s_sem.at[OT], r_sem.at[OT]), {"tm": tm_peer(d)}
        )

    wait(p_buf.at[c], r_sem.at[PF])

    rows = lax.broadcasted_iota(jnp.int32, (members, members), 0)
    cols = lax.broadcasted_iota(jnp.int32, (members, members), 1)
    identity = jnp.where(rows == cols, 1.0, 0.0).astype(f32)

    def block(b):
        return jnp.concatenate([p_buf[0, b], p_buf[1, b]], axis=0)

    later = jnp.where(n_tm - 1 > me, block(n_tm - 1), identity)
    for b in reversed(range(n_tm // 2, n_tm - 1)):
        later = mm(jnp.where(b > me, block(b), identity), later)
    prod_out[times] = later
    hand_round(0)
    later = prod_out[times]
    for b in reversed(range(1, n_tm // 2)):
        later = mm(jnp.where(b > me, block(b), identity), later)
    prod_out[times] = later
    for k in range(1, own):
        hand_round(k)
    later = prod_out[times]
    pre_out[0] = identity
    for b in range(n_tm - 1):
        p_out[b] = jnp.where(b < me, block(b), identity)
    for t in range(times):
        prod_out[t] = mm(suf[t], later)

    def big_products(first, last):
        for t in range(first, last):
            factor = prod_out[t].astype(bf16)
            sm_v[t] = lax.dot_general(
                factor, e_v[t], (((0,), (0,)), ((), ())), preferred_element_type=f32
            ).astype(bf16)
            eg_v[t] = jnp.dot(factor, c_v[t], preferred_element_type=f32).astype(bf16)

    big_products(0, times // 2)
    forward_totals(0)
    big_products(times // 2, 3 * times // 4)
    wait(ot_buf.at[c, pl.ds(0, n_tm - 1)], r_sem.at[OT])
    send(ot_buf.at[c], ot_buf.at[c], (s_sem.at[OF], r_sem.at[OF]), {"space": partner})
    for k in range(1, own):
        forward_totals(k)
    big_products(3 * times // 4, times)
    wait(ot_buf.at[c], r_sem.at[OF])
    for b in range(n_tm - 1):
        ot_out[b] = jnp.where(
            b < me, jnp.concatenate([ot_buf[0, b], ot_buf[1, b]], axis=0), 0.0
        )
    for k in range(own):
        wait(lt_fin.at[k, c], lf_r.at[k])
    for k in range(own):
        for q in range(n_y):
            for core in range(2):
                lt_out[2 * (k * n_y + q) + core] = lt_fin[k, core, q]
    wait(p_buf.at[c, pl.ds(0, n_tm - 1)], s_sem.at[PB])
    wait(p_buf.at[c], s_sem.at[PF])
    wait(ltp.at[c], s_sem.at[LP])
    wait(lt_ry, s_sem.at[LY])
    wait(lt_ry, s_sem.at[LA])
    wait(lt_fin.at[:, c], s_sem.at[LF])
    wait(ot_rx, s_sem.at[OR])
    wait(ot_buf.at[c, pl.ds(0, n_tm - 1)], s_sem.at[OT])
    wait(ot_buf.at[c], s_sem.at[OF])


def output_kernel(
    times, members, scale,
    sm_v, eg_v, lt, pre, prod, blocks, leaving,
    sm_hbm, eg_hbm, tg_hbm,
    tg, carry, sems, tg_sem,
):
    copies = []

    def write(q):
        part = pl.ds(q * (times // 4), times // 4)
        for k, (src, dst) in enumerate(((sm_v, sm_hbm), (eg_v, eg_hbm))):
            copy = pltpu.make_async_copy(src.at[part], dst.at[part], sems.at[k, q])
            copy.start()
            copies.append(copy)

    for q in range(4):
        write(q)
    last = blocks.shape[0]
    entering = leaving[0]
    for k, (first, stop) in enumerate(((1, last // 2), (last // 2, last))):
        for b in range(first, stop):
            entering = mm(entering, blocks[b]) + leaving[b]
        carry[...] = entering
        copies[k].wait()
        entering = carry[...]
    for q in range(2):
        part = pl.ds(q * (times // 2), times // 2)
        entering = carry[...]
        for t in range(q * (times // 2), (q + 1) * (times // 2)):
            total = unpack(lt[t], members) + mm(entering, pre[t])
            tg[t] = mm(prod[t + 1], total).T * scale
        copies[2 + q].wait()
        copy = pltpu.make_async_copy(tg.at[part], tg_hbm.at[part], tg_sem.at[q])
        copy.start()
        copies.append(copy)
    for copy in copies[4:]:
        copy.wait()


def shards(n_tm, n_sp, ensembles, cotangents, transforms):
    times, members, cells = ensembles.shape
    half = members // 2
    n_y = n_sp // 2
    per_core = times // 2
    own = per_core // n_y
    square = (members, members)
    halves = (half, members)
    packed = (half + members // 5, 128)
    anywhere = pl.BlockSpec(memory_space=pl.ANY)
    vmem = pl.BlockSpec(memory_space=pltpu.VMEM)
    dma = pltpu.SemaphoreType.DMA
    shape = jax.ShapeDtypeStruct
    big = shape((times, members, cells), bf16)
    stack = shape((times,) + square, f32)
    chain = shape((n_tm - 1,) + square, f32)
    passed = pl.pallas_call(
        functools.partial(exchange_kernel, n_tm, n_sp, times, members),
        out_shape=[
            big, big, shape((times,) + packed, f32), stack,
            shape((times + 1,) + square, f32), chain, chain,
        ],
        in_specs=[anywhere] * 3,
        out_specs=[vmem] * 7,
        scratch_shapes=[
            pltpu.VMEM((times, members, cells), bf16),
            pltpu.VMEM((times, members, cells), bf16),
            pltpu.VMEM((times,) + square, f32),
            pltpu.VMEM((2,) + halves, f32),
            pltpu.VMEM((2, n_tm) + halves, f32),
            pltpu.VMEM((2, per_core) + packed, f32),
            pltpu.VMEM((per_core,) + packed, f32),
            pltpu.VMEM((per_core,) + packed, f32),
            pltpu.VMEM((own, n_y - 1) + packed, f32),
            pltpu.VMEM((own, 2, n_y) + packed, f32),
            pltpu.VMEM((2,) + halves, f32),
            pltpu.VMEM((n_sp - 1,) + halves, f32),
            pltpu.VMEM((2, n_tm) + halves, f32),
            pltpu.VMEM((times,) + square, f32),
            pltpu.VMEM((times // 4, 5) + square, f32),
            pltpu.VMEM((times,) + square, f32),
            pltpu.VMEM(square, f32),
            dma((11,)),
            dma((9,)), dma((5,)), dma((own,)), dma((own,)), dma((own,)), dma((own,)),
        ],
        compiler_params=pltpu.CompilerParams(
            collective_id=0, has_side_effects=True, vmem_limit_bytes=34 * 2**20
        ),
        name="exchange",
    )(*(pltpu.with_memory_space_constraint(a, pltpu.HBM) for a in (ensembles, cotangents, transforms)))
    scale = 1.0 / math.sqrt(cells * n_sp * times * n_tm)
    return pl.pallas_call(
        functools.partial(output_kernel, times, members, scale),
        out_shape=[big, big, stack],
        in_specs=[vmem] * 7,
        out_specs=[anywhere] * 3,
        scratch_shapes=[
            pltpu.VMEM((times,) + square, f32), pltpu.VMEM(square, f32), dma((2, 4)), dma((2,)),
        ],
        compiler_params=pltpu.CompilerParams(vmem_limit_bytes=8 * 2**20),
        name="outputs",
    )(*passed)


def solution(mesh):
    specs = (P("tm", None, "space"), P("tm", None, "space"), P("tm", None, None))
    return jax.shard_map(
        functools.partial(shards, mesh.shape["tm"], mesh.shape["space"]),
        mesh=mesh,
        in_specs=specs,
        out_specs=specs,
        check_vma=False,
    )
```

time: 41.7 us -> 31.6 us (0.76)
  Pallas kernels: 40.8 us -> 30.9 us
    pallas_call x1, Pallas kernels: 33.7 us -> 25.6 us  [shards(): pl.pallas_call(functools.partial(exchange_kernel, n_tm, n_sp, times, memb...]
    pallas_call x1, Pallas kernels: 7.08 us -> 5.28 us  [shards(): pl.pallas_call(functools.partial(output_kernel, times, members, scale), o...]
where the time goes in v1:
time: 31.6 us; the launch traced here: 31.5 us
  Pallas kernels  30.9 us (98%)
  between operations  0.64 us (2%)
    pallas_call x1, Pallas kernels, shards(): pl.pallas_call(functools.partial(exchange_kernel, n_tm, n_sp, times, memb...  25.6 us
    pallas_call x1, Pallas kernels, shards(): pl.pallas_call(functools.partial(output_kernel, times, members, scale), o...  5.28 us

profile of v1, /device:TPU:1, one launch (start us, length us, event | category | flops | bytes accessed | tf_op | source)
XLA Modules:
  0.0 31.5 jit_solution(4384320856540582189)
XLA Ops:
  0.6 25.6 %exchange.1 = (bf16[16,80,2048]{2,1,0:T(8,128)(2,1)S(1)}, bf16[16,80,2048]{2,1,0:T(8,128)(2,1)S(1)}, f32[16,56,128]{2,1,0:T(8,128)S(1)}, f32[16,80,80]{2,1,0:T(8...) custom-call(bf16[16,80,2048]{2,1,0:T(8,128)(2,1)} %e_hbm.1, ...), custom_call_target="tpu_custom_call" | custom-call | tf_op jit(solution)/shard_map/exchange/pallas_call | solution.py:357
  26.2 5.3 %outputs.1 = (bf16[16,80,2048]{2,1,0:T(8,128)(2,1)}, bf16[16,80,2048]{2,1,0:T(8,128)(2,1)}, f32[16,80,80]{2,1,0:T(8,128)}) custom-call(bf16[16,80,2048]{2,1,0:T(8,128)(2,1)S(1)} %get-tuple-element.10.sm_v, bf16[16,80,2048]{2,1,0:T(8,128)(2,1)S(1)} %get-tuple-element.11.eg_v, f32[16,56,128]{2,1,0:T(8,128)S(1)} %get-tuple-element.12.lt, ...), custom_call_target="tpu_custom_call" | custom-call | tf_op jit(solution)/shard_map/outputs/pallas_call | solution.py:392

commit v2 on v1

--- a/solution.py
+++ b/solution.py
@@ -9,7 +9,7 @@
 from jax.sharding import PartitionSpec as P
 
 MESH = pl.DeviceIdType.MESH
-PB, PF, OR, OT, OF, LP, LY, LA, LF = range(9)
+PB, PF, OR, OT, OF, OC, LP, LY, LA, LF = range(10)
 f32 = jnp.float32
 bf16 = jnp.bfloat16
 
@@ -20,13 +20,11 @@
     )
 
 
-def group_scans(tr, groups):
-    heads, tails = [], []
-    for g in range(groups):
-        w = [tr[4 * g + i] for i in range(4)]
-        w01, w23 = mm(w[0], w[1]), mm(w[2], w[3])
-        heads.append((w[0], w01, mm(w01, w[2]), mm(w01, w23)))
-        tails.append((None, mm(w[1], w23), w23, w[3]))
+def group_scans(tr, g):
+    w = [tr[4 * g + i] for i in range(4)]
+    w01, w23 = mm(w[0], w[1]), mm(w[2], w[3])
+    heads = (w[0], w01, mm(w01, w[2]), mm(w01, w23))
+    tails = (None, mm(w[1], w23), w23, w[3])
     return heads, tails
 
 
@@ -81,7 +79,7 @@
     n_tm, n_sp, times, members,
     e_hbm, c_hbm, t_hbm,
     sm_v, eg_v, lt_out, pre_out, prod_out, p_out, ot_out,
-    e_v, c_v, tr, p_own, p_buf, ltp, lt_rx, lt_core, lt_ry, lt_fin, ot_own, ot_rx, ot_buf, suf, scan_buf, gram, carry,
+    e_v, c_v, tr, p_own, p_buf, ltp, lt_rx, lt_core, lt_ry, lt_fin, ot_own, ot_rx, ot_core, ot_buf, suf, scan_buf, gram, carry,
     in_sem, s_sem, r_sem, lp_r, ly_r, la_r, lf_r,
 ):
     half = members // 2
@@ -197,20 +195,24 @@
     leaving = mm(carry[...], tr[times - 1])
     ot_own[0] = leaving[:half]
     ot_own[1] = leaving[half:]
-    for d in range(1, n_sp):
-        peer = sp_peer(d)
-        send(
-            ot_own.at[lax.rem(peer, 2)], ot_rx.at[d - 1], (s_sem.at[OR], r_sem.at[OR]),
-            {"space": peer},
-        )
-
+    send(ot_own.at[1 - c], ot_rx.at[n_y - 1], (s_sem.at[OC], r_sem.at[OC]), {"space": partner})
+
+    def scan_groups(first, last):
+        for g in range(first, last):
+            heads, tails = group_scans(tr, g)
+            for i in range(1, 4):
+                scan_buf[g, i - 1] = heads[i]
+            for i in range(1, 3):
+                scan_buf[g, 2 + i] = tails[i]
+
+    scan_groups(0, times // 8)
+    wait(ot_own.at[0], r_sem.at[OC])
+    ot_core[...] = ot_own[c] + ot_rx[n_y - 1]
+    for d in range(1, n_y):
+        q = lax.rem(y + d, n_y)
+        send(ot_core, ot_rx.at[d - 1], (s_sem.at[OR], r_sem.at[OR]), {"space": 2 * q + c})
     reduce_cores(0)
-    heads, tails = group_scans(tr, times // 4)
-    for g in range(times // 4):
-        for i in range(1, 4):
-            scan_buf[g, i - 1] = heads[g][i]
-        for i in range(1, 3):
-            scan_buf[g, 2 + i] = tails[g][i]
+    scan_groups(times // 8, times // 4)
     for k in range(1, own):
         reduce_cores(k)
     heads = [
@@ -224,9 +226,9 @@
     wait(p_buf.at[c, pl.ds(0, n_tm - 1)], r_sem.at[PB])
     send(p_buf.at[c], p_buf.at[c], (s_sem.at[PF], r_sem.at[PF]), {"space": partner})
 
-    wait(ot_rx, r_sem.at[OR])
-    summed = ot_own[c]
-    for d in range(1, n_sp):
+    wait(ot_rx.at[pl.ds(0, n_y - 1)], r_sem.at[OR])
+    summed = ot_core[...]
+    for d in range(1, n_y):
         summed = summed + ot_rx[d - 1]
     ot_buf[c, me] = summed
     for d in range(1, n_tm):
@@ -277,24 +279,25 @@
     for k in range(1, own):
         forward_totals(k)
     big_products(3 * times // 4, times)
-    wait(ot_buf.at[c], r_sem.at[OF])
-    for b in range(n_tm - 1):
-        ot_out[b] = jnp.where(
-            b < me, jnp.concatenate([ot_buf[0, b], ot_buf[1, b]], axis=0), 0.0
-        )
     for k in range(own):
         wait(lt_fin.at[k, c], lf_r.at[k])
     for k in range(own):
         for q in range(n_y):
             for core in range(2):
                 lt_out[2 * (k * n_y + q) + core] = lt_fin[k, core, q]
+    wait(ot_buf.at[c], r_sem.at[OF])
+    for b in range(n_tm - 1):
+        ot_out[b] = jnp.where(
+            b < me, jnp.concatenate([ot_buf[0, b], ot_buf[1, b]], axis=0), 0.0
+        )
     wait(p_buf.at[c, pl.ds(0, n_tm - 1)], s_sem.at[PB])
     wait(p_buf.at[c], s_sem.at[PF])
     wait(ltp.at[c], s_sem.at[LP])
     wait(lt_ry, s_sem.at[LY])
     wait(lt_ry, s_sem.at[LA])
     wait(lt_fin.at[:, c], s_sem.at[LF])
-    wait(ot_rx, s_sem.at[OR])
+    wait(ot_rx.at[pl.ds(0, n_y - 1)], s_sem.at[OR])
+    wait(ot_own.at[0], s_sem.at[OC])
     wait(ot_buf.at[c, pl.ds(0, n_tm - 1)], s_sem.at[OT])
     wait(ot_buf.at[c], s_sem.at[OF])
 
@@ -318,9 +321,13 @@
         write(q)
     last = blocks.shape[0]
     entering = leaving[0]
+    tg[0] = unpack(lt[0], members)
+    for t in range(last, times):
+        tg[t] = unpack(lt[t], members)
     for k, (first, stop) in enumerate(((1, last // 2), (last // 2, last))):
         for b in range(first, stop):
             entering = mm(entering, blocks[b]) + leaving[b]
+            tg[b] = unpack(lt[b], members)
         carry[...] = entering
         copies[k].wait()
         entering = carry[...]
@@ -328,7 +335,7 @@
         part = pl.ds(q * (times // 2), times // 2)
         entering = carry[...]
         for t in range(q * (times // 2), (q + 1) * (times // 2)):
-            total = unpack(lt[t], members) + mm(entering, pre[t])
+            total = tg[t] + mm(entering, pre[t])
             tg[t] = mm(prod[t + 1], total).T * scale
         copies[2 + q].wait()
         copy = pltpu.make_async_copy(tg.at[part], tg_hbm.at[part], tg_sem.at[q])
@@ -374,14 +381,15 @@
             pltpu.VMEM((own, n_y - 1) + packed, f32),
             pltpu.VMEM((own, 2, n_y) + packed, f32),
             pltpu.VMEM((2,) + halves, f32),
-            pltpu.VMEM((n_sp - 1,) + halves, f32),
+            pltpu.VMEM((n_y,) + halves, f32),
+            pltpu.VMEM(halves, f32),
             pltpu.VMEM((2, n_tm) + halves, f32),
             pltpu.VMEM((times,) + square, f32),
             pltpu.VMEM((times // 4, 5) + square, f32),
             pltpu.VMEM((times,) + square, f32),
             pltpu.VMEM(square, f32),
             dma((11,)),
-            dma((9,)), dma((5,)), dma((own,)), dma((own,)), dma((own,)), dma((own,)),
+            dma((10,)), dma((6,)), dma((own,)), dma((own,)), dma((own,)), dma((own,)),
         ],
         compiler_params=pltpu.CompilerParams(
             collective_id=0, has_side_effects=True, vmem_limit_bytes=34 * 2**20

time: 31.6 us -> 31.3 us (level)
  Pallas kernels: 30.9 us -> 30.5 us
where the time goes in v2:
time: 31.3 us; the launch traced here: 31.2 us
  Pallas kernels  30.5 us (97%)
  between operations  0.64 us (2%)
    pallas_call x1, Pallas kernels, shards(): pl.pallas_call(functools.partial(exchange_kernel, n_tm, n_sp, times, memb...  25.4 us
    pallas_call x1, Pallas kernels, shards(): pl.pallas_call(functools.partial(output_kernel, times, members, scale), o...  5.11 us

profile of v2, /device:TPU:1, one launch (start us, length us, event | category | flops | bytes accessed | tf_op | source)
XLA Modules:
  0.0 31.2 jit_solution(6181924427615518338)
XLA Ops:
  0.6 25.4 %exchange.1 = (bf16[16,80,2048]{2,1,0:T(8,128)(2,1)S(1)}, bf16[16,80,2048]{2,1,0:T(8,128)(2,1)S(1)}, f32[16,56,128]{2,1,0:T(8,128)S(1)}, f32[16,80,80]{2,1,0:T(8...) custom-call(bf16[16,80,2048]{2,1,0:T(8,128)(2,1)} %e_hbm.1, ...), custom_call_target="tpu_custom_call" | custom-call | tf_op jit(solution)/shard_map/exchange/pallas_call | solution.py:364
  26.1 5.1 %outputs.1 = (bf16[16,80,2048]{2,1,0:T(8,128)(2,1)}, bf16[16,80,2048]{2,1,0:T(8,128)(2,1)}, f32[16,80,80]{2,1,0:T(8,128)}) custom-call(bf16[16,80,2048]{2,1,0:T(8,128)(2,1)S(1)} %get-tuple-element.10.sm_v, bf16[16,80,2048]{2,1,0:T(8,128)(2,1)S(1)} %get-tuple-element.11.eg_v, f32[16,56,128]{2,1,0:T(8,128)S(1)} %get-tuple-element.12.lt, ...), custom_call_target="tpu_custom_call" | custom-call | tf_op jit(solution)/shard_map/outputs/pallas_call | solution.py:400
